TPU v7x, 32 devices: a whole 2x2x4 slice. The times are simulated.
32 devices in a mesh: row: 4 (over y, core), col: 8 (over z, x).
Axes of the slice: x: 2, y: 2, z: 4, core: 2. Of those that a mesh axis runs over, the one named last changes fastest.
Arguments:
- orbitals: bfloat16 [4, 8, 1024, 512], P('row', 'col'), may hold values from -6 to 6
- tiles: bfloat16 [4, 8, 60, 128, 128], P('row', 'col'), may hold values from -0.1875 to 0.1875
- tile_rows: int32 [4, 8, 60], P('row', 'col'), may hold values from 0 to 7, as said below
- tile_cols: int32 [4, 8, 60], P('row', 'col'), may hold values from 0 to 13
Outputs:
- product: bfloat16 [4, 8, 1024, 512], P('row', 'col')
Inputs may be any that keep to these rules, and one draw needn't show every extreme that they name: The pairs (tile_rows, tile_cols) of one grid position are distinct, and tile_rows <= tile_cols wherever tile_cols < 8.
All inputs are finite; a program needn't handle non-finite values.
Results may differ from a plain program's by a relative error of at most 0.001.
Values may be sent and summed in bfloat16 or wider, within the bound.
No kernel may reach another device: no remote copies, remote signals or barrier semaphores. Data moves between devices by JAX's collectives and lax.ppermute only.
A program may use at most 64 MiB of HBM per device.

v0:
```python
import jax
import jax.numpy as jnp
from jax import lax
from jax.experimental import pallas as pl
from jax.experimental.pallas import tpu as pltpu
from jax.sharding import PartitionSpec as P


BS = 128
CB = 8
RIM = 2
SCALE = 16.0


VMEM = pl.BlockSpec(memory_space=pltpu.VMEM)
ANY = pl.BlockSpec(memory_space=pl.ANY)
F32, BF16 = jnp.float32, jnp.bfloat16


def shifted(shard, axis, by):
    size = lax.axis_size(axis)
    return lax.ppermute(shard, axis, [(i, (i + by) % size) for i in range(size)])


def here(x):
    return pltpu.with_memory_space_constraint(x, pltpu.VMEM)


def there(x):
    return pltpu.with_memory_space_constraint(x, pltpu.HBM)


def call(kernel, out_shape, operands, in_specs=None, **options):
    many = isinstance(out_shape, tuple)
    if in_specs is None:
        in_specs = [VMEM] * len(operands)
        operands = [here(x) for x in operands]
    return pl.pallas_call(
        kernel,
        out_shape=out_shape,
        in_specs=in_specs,
        compiler_params=pltpu.CompilerParams(vmem_limit_bytes=24 << 20),
        **{"out_specs": (VMEM,) * len(out_shape) if many else VMEM, **options},
    )(*operands)


def dot(a, b):
    return jnp.dot(a, b, preferred_element_type=F32)


def transposed_dot(a, b):
    return lax.dot_general(a, b, (((0,), (0,)), ((), ())), preferred_element_type=F32)


def rim_columns(k):
    first = (CB + k * RIM) * BS
    return slice(first, first + RIM * BS)


def gather_kernel(rows_hbm, cols_hbm, tiles_hbm, owned_hbm, dense, owned, rim, to_diag, tiles, rows, cols, sems):
    copies = [
        pltpu.make_async_copy(rows_hbm, rows, sems.at[0]),
        pltpu.make_async_copy(cols_hbm, cols, sems.at[1]),
        pltpu.make_async_copy(tiles_hbm, tiles, sems.at[2]),
        pltpu.make_async_copy(owned_hbm, owned, sems.at[3]),
    ]
    for copy in copies:
        copy.start()
    dense[...] = jnp.zeros_like(dense)
    for copy in copies[:3]:
        copy.wait()
    for t in range(tiles.shape[0]):
        row, col = rows[0, 0, t], cols[0, 0, t]
        dense[pl.ds(pl.multiple_of(row * BS, BS), BS), pl.ds(pl.multiple_of(col * BS, BS), BS)] = tiles[t]
    copies[3].wait()
    rim[...] = owned[:RIM * BS, :]
    to_diag[...] = transposed_dot(dense[:, rim_columns(2)], owned[...])


def mirror_kernel(dense, owned, to_col, to_row):
    to_row[...] = transposed_dot(dense[:, rim_columns(1)], owned[...])
    to_col[...] = transposed_dot(dense[:, rim_columns(0)], owned[...])


def own_kernel(dense, owned, total, square):
    for i in range(CB):
        block = slice(i * BS, (i + 1) * BS)
        square[block, i * BS:CB * BS] = dense[block, i * BS:CB * BS]
        for j in range(i + 1, CB):
            square[j * BS:(j + 1) * BS, block] = dense[block, j * BS:(j + 1) * BS].T
    total[...] = dot(square[...], owned[...])


def beside_kernel(total, dense, beside, below, more):
    more[...] = total[...] + dot(dense[:, rim_columns(0)], beside[...]) + dot(dense[:, rim_columns(1)], below[...])


def finish_kernel(total, dense, corner, from_row, from_col, out):
    acc = total[...] + dot(dense[:, rim_columns(2)], corner[...])
    out[RIM * BS:, :] = acc[RIM * BS:].astype(out.dtype)
    out[:RIM * BS, :] = (acc[:RIM * BS] + from_row[...] + from_col[...]).astype(out.dtype)


def inner_body(orbitals, tiles, tile_rows, tile_cols):
    occ = orbitals.shape[-1]
    rim_rows = RIM * BS
    owned_hbm = orbitals.reshape(CB * BS, occ)
    stored = tiles.reshape(-1, BS, BS)
    part = pltpu.VMEM((rim_rows, occ), F32)
    whole = pltpu.VMEM((CB * BS, occ), F32)
    dense, owned, rim, to_diag = call(
        gather_kernel,
        (pltpu.VMEM((CB * BS, (CB + 3 * RIM) * BS), BF16), pltpu.VMEM((CB * BS, occ), BF16), pltpu.VMEM((rim_rows, occ), BF16), part),
        [there(x) for x in (tile_rows, tile_cols, stored, owned_hbm)],
        in_specs=[ANY] * 4,
        scratch_shapes=[
            pltpu.VMEM(stored.shape, BF16),
            pltpu.SMEM(tile_rows.shape, jnp.int32),
            pltpu.SMEM(tile_cols.shape, jnp.int32),
            pltpu.SemaphoreType.DMA((4,)),
        ],
    )
    to_col, to_row = call(mirror_kernel, (part, part), (dense, owned))
    enc = lambda x: (x * SCALE).astype(jnp.float16)
    dec = lambda x: x.astype(F32) * (1 / SCALE)
    from_diag = shifted(enc(to_diag), "row", 1)
    beside = shifted(rim, "col", -1)
    from_row = shifted(enc(to_row), "row", 1)
    below = shifted(rim, "row", -1)
    corner = shifted(beside, "row", -1)
    from_col = shifted(enc(to_col + dec(from_diag)), "col", 1)
    total = call(own_kernel, whole, (dense, owned), scratch_shapes=[pltpu.VMEM((CB * BS, CB * BS), BF16)])
    total = call(beside_kernel, whole, (total, dense, beside, below))
    out = call(finish_kernel, jax.ShapeDtypeStruct((CB * BS, occ), BF16), (total, dense, corner, dec(from_row), dec(from_col)))
    return out.reshape(orbitals.shape)


def solution(mesh):
    return jax.shard_map(
        inner_body,
        mesh=mesh,
        in_specs=(
            P("row", "col", None, None),
            P("row", "col", None, None, None),
            P("row", "col", None),
            P("row", "col", None),
        ),
        out_specs=P("row", "col", None, None),
        check_vma=False,
    )
```

profile of v0, /device:TPU:0, one launch (start us, length us, event | category | flops | bytes accessed | tf_op | source)
XLA Modules:
  0.0 24.1 jit_solution(2092243941266058998)
XLA Ops:
  0.0 2.4 %shard_map.46 = (bf16[1024,1792]{1,0:T(8,128)(2,1)S(1)}, bf16[1024,512]{1,0:T(8,128)(2,1)S(1)}, bf16[256,512]{1,0:T(8,128)(2,1)S(1)}, f32[256,512]{1,0:T(8,128)S(1)}) custom-call(s32[1,1,60]{2,1,0:T(1,128)} %rows_hbm.1, s32[1,1,60]{2,1,0:T(1,128)} %cols_hbm.1, bf16[60,128,128]{2,1,0:T(8,128)(2,1)} %bitcast.3, bf16[1024,512]{1,0:T(8,128)(2,1)} %bitcast.4), custom_call_target="tpu_custom_call" | custom-call | tf_op jit(solution)/shard_map/pallas_call | solution.py:38
  2.5 0.5 %collective-permute-start.4 = (f16[256,512]{1,0:T(8,128)(2,1)S(1)}, f16[256,512]{1,0:T(8,128)(2,1)S(1)}, u32[]{:S(2)}, u32[]{:S(2)}) collective-permute-start(f16[256,512]{1,0:T(8,128)(2,1)S(1)} %multiply_convert_fusion.1), channel_id=1, source_target_pairs={{0,8},{8,16},{16,24},{24,0},{1,9},{9,17},{17,25},{25,1},{2,10},{10... | collective-permute-start | bytes 786440 | tf_op jit(solution)/shard_map/ppermute | solution.py:22
  3.1 2.0 %collective-permute-start.1 = (bf16[256,512]{1,0:T(8,128)(2,1)S(1)}, bf16[256,512]{1,0:T(8,128)(2,1)S(1)}, u32[]{:S(2)}, u32[]{:S(2)}) collective-permute-start(bf16[256,512]{1,0:T(8,128)(2,1)S(1)} %get-tuple-element.13), channel_id=1, source_target_pairs={{0,24},{8,0},{16,8},{24,16},{1,25},{9,1},{17,9},{25,17},{2,26},{10... | collective-permute-start | bytes 786440 | tf_op jit(solution)/shard_map/ppermute | solution.py:22
  5.1 5.2 %collective-permute-start = (bf16[256,512]{1,0:T(8,128)(2,1)S(1)}, bf16[256,512]{1,0:T(8,128)(2,1)S(1)}, u32[]{:S(2)}, u32[]{:S(2)}) collective-permute-start(bf16[256,512]{1,0:T(8,128)(2,1)S(1)} %get-tuple-element.13), channel_id=1, source_target_pairs={{0,7},{1,0},{2,1},{3,2},{4,3},{5,4},{6,5},{7,6},{8,15},{9,8},{10,9... | collective-permute-start | bytes 786440 | tf_op jit(solution)/shard_map/ppermute | solution.py:22
  10.3 0.7 %shard_map.49 = (f32[256,512]{1,0:T(8,128)S(1)}, f32[256,512]{1,0:T(8,128)S(1)}) custom-call(bf16[1024,1792]{1,0:T(8,128)(2,1)S(1)} %get-tuple-element.11.dense, bf16[1024,512]{1,0:T(8,128)(2,1)S(1)} %get-tuple-element.12.owned), custom_call_target="tpu_custom_call" | custom-call | tf_op jit(solution)/shard_map/pallas_call | solution.py:38
  11.1 0.1 collective-permute-start.3
  11.2 0.0 collective-permute-done.4
  11.2 0.1 multiply_convert_fusion
  11.3 1.2 %collective-permute-start.5 = (f16[256,512]{1,0:T(8,128)(2,1)S(1)}, f16[256,512]{1,0:T(8,128)(2,1)S(1)}, u32[]{:S(2)}, u32[]{:S(2)}) collective-permute-start(f16[256,512]{1,0:T(8,128)(2,1)S(1)} %multiply_convert_fusion), channel_id=1, source_target_pairs={{0,1},{1,2},{2,3},{3,4},{4,5},{5,6},{6,7},{7,0},{8,9},{9,10},{10,1... | collective-permute-start | bytes 786440 | tf_op jit(solution)/shard_map/ppermute | solution.py:22
  12.5 1.3 %shard_map.47.total = f32[1024,512]{1,0:T(8,128)S(1)} custom-call(bf16[1024,1792]{1,0:T(8,128)(2,1)S(1)} %get-tuple-element.11.dense, bf16[1024,512]{1,0:T(8,128)(2,1)S(1)} %get-tuple-element.12.owned), custom_call_target="tpu_custom_call" | custom-call | tf_op jit(solution)/shard_map/pallas_call | solution.py:38
  13.7 2.2 %collective-permute-done.beside = bf16[256,512]{1,0:T(8,128)(2,1)S(1)} collective-permute-done((bf16[256,512]{1,0:T(8,128)(2,1)S(1)}, bf16[256,512]{1,0:T(8,128)(2,1)S(1)}, u32[]{:S(2)}, u32[]{:S(2)}) %collective-permute-start) | collective-permute-done | bytes 262176 | tf_op jit(solution)/shard_map/ppermute | solution.py:22
  15.9 0.0 collective-permute-start.2
  15.9 1.0 %collective-permute-done.3 = f16[256,512]{1,0:T(8,128)(2,1)S(1)} collective-permute-done((f16[256,512]{1,0:T(8,128)(2,1)S(1)}, f16[256,512]{1,0:T(8,128)(2,1)S(1)}, u32[]{:S(2)}, u32[]{:S(2)}) %collective-permute-start.3) | collective-permute-done | bytes 262176 | tf_op jit(solution)/shard_map/ppermute | solution.py:22
  17.0 0.1 convert_multiply_fusion.1.from_row
  17.0 0.0 collective-permute-done.1.below
  17.0 0.7 %shard_map.48.total = f32[1024,512]{1,0:T(8,128)S(1)} custom-call(f32[1024,512]{1,0:T(8,128)S(1)} %shard_map.47.total, bf16[1024,1792]{1,0:T(8,128)(2,1)S(1)} %get-tuple-element.11.dense, bf16[256,512]{1,0:T(8,128)(2,1)S(1)} %collective-permute-done.beside, bf16[256,512]{1,0:T(8,128)(2,1)S(1)} %collective-permute-done.1.below), custom_call_target="tpu_custom_call" | custom-call | tf_op jit(solution)/shard_map/pallas_call | solution.py:38
  17.7 4.8 %collective-permute-done.5 = f16[256,512]{1,0:T(8,128)(2,1)S(1)} collective-permute-done((f16[256,512]{1,0:T(8,128)(2,1)S(1)}, f16[256,512]{1,0:T(8,128)(2,1)S(1)}, u32[]{:S(2)}, u32[]{:S(2)}) %collective-permute-start.5) | collective-permute-done | bytes 262176 | tf_op jit(solution)/shard_map/ppermute | solution.py:22
  22.6 0.1 convert_multiply_fusion.from_col
  22.6 0.0 collective-permute-done.2.corner
  22.7 1.4 %shard_map.50 = bf16[1024,512]{1,0:T(8,128)(2,1)} custom-call(f32[1024,512]{1,0:T(8,128)S(1)} %shard_map.48.total, bf16[1024,1792]{1,0:T(8,128)(2,1)S(1)} %get-tuple-element.11.dense, bf16[256,512]{1,0:T(8,128)(2,1)S(1)} %collective-permute-done.2.corner, f32[256,512]{1,0:T(8,128)S(1)} %convert_multiply_fusion.1.from_row, ...), custom_call_target="tpu_custom_call" | custom-call | tf_op jit(solution)/shard_map/pallas_call | solution.py:38
  (2 shorter events, 0.1 us)
Async XLA Ops:
  2.5 8.7 %collective-permute-start.4 = (f16[256,512]{1,0:T(8,128)(2,1)S(1)}, f16[256,512]{1,0:T(8,128)(2,1)S(1)}, u32[]{:S(2)}, u32[]{:S(2)}) collective-permute-start(f16[256,512]{1,0:T(8,128)(2,1)S(1)} %multiply_convert_fusion.1), channel_id=1, source_target_pairs={{0,8},{8,16},{16,24},{24,0},{1,9},{9,17},{17,25},{25,1},{2,10},{10... | collective-permute-start | bytes 786440 | tf_op jit(solution)/shard_map/ppermute | solution.py:22
  3.1 14.0 %collective-permute-start.1 = (bf16[256,512]{1,0:T(8,128)(2,1)S(1)}, bf16[256,512]{1,0:T(8,128)(2,1)S(1)}, u32[]{:S(2)}, u32[]{:S(2)}) collective-permute-start(bf16[256,512]{1,0:T(8,128)(2,1)S(1)} %get-tuple-element.13), channel_id=1, source_target_pairs={{0,24},{8,0},{16,8},{24,16},{1,25},{9,1},{17,9},{25,17},{2,26},{10... | collective-permute-start | bytes 786440 | tf_op jit(solution)/shard_map/ppermute | solution.py:22
  5.1 10.9 %collective-permute-start = (bf16[256,512]{1,0:T(8,128)(2,1)S(1)}, bf16[256,512]{1,0:T(8,128)(2,1)S(1)}, u32[]{:S(2)}, u32[]{:S(2)}) collective-permute-start(bf16[256,512]{1,0:T(8,128)(2,1)S(1)} %get-tuple-element.13), channel_id=1, source_target_pairs={{0,7},{1,0},{2,1},{3,2},{4,3},{5,4},{6,5},{7,6},{8,15},{9,8},{10,9... | collective-permute-start | bytes 786440 | tf_op jit(solution)/shard_map/ppermute | solution.py:22
  11.1 5.8 %collective-permute-start.3 = (f16[256,512]{1,0:T(8,128)(2,1)S(1)}, f16[256,512]{1,0:T(8,128)(2,1)S(1)}, u32[]{:S(2)}, u32[]{:S(2)}) collective-permute-start(f16[256,512]{1,0:T(8,128)(2,1)S(1)} %multiply_convert_fusion.2), channel_id=1, source_target_pairs={{0,8},{8,16},{16,24},{24,0},{1,9},{9,17},{17,25},{25,1},{2,10},{10... | collective-permute-start | bytes 786440 | tf_op jit(solution)/shard_map/ppermute | solution.py:22
  11.3 11.3 %collective-permute-start.5 = (f16[256,512]{1,0:T(8,128)(2,1)S(1)}, f16[256,512]{1,0:T(8,128)(2,1)S(1)}, u32[]{:S(2)}, u32[]{:S(2)}) collective-permute-start(f16[256,512]{1,0:T(8,128)(2,1)S(1)} %multiply_convert_fusion), channel_id=1, source_target_pairs={{0,1},{1,2},{2,3},{3,4},{4,5},{5,6},{6,7},{7,0},{8,9},{9,10},{10,1... | collective-permute-start | bytes 786440 | tf_op jit(solution)/shard_map/ppermute | solution.py:22
  15.9 6.7 %collective-permute-start.2 = (bf16[256,512]{1,0:T(8,128)(2,1)S(1)}, bf16[256,512]{1,0:T(8,128)(2,1)S(1)}, u32[]{:S(2)}, u32[]{:S(2)}) collective-permute-start(bf16[256,512]{1,0:T(8,128)(2,1)S(1)} %collective-permute-done.beside), channel_id=1, source_target_pairs={{0,24},{8,0},{16,8},{24,16},{1,25},{9,1},{17,9},{25,17},{2,26},{10... | collective-permute-start | bytes 786440 | tf_op jit(solution)/shard_map/ppermute | solution.py:22
where the time goes:
time: 24.2 us; the launch traced here: 24.1 us
  starting transfers between devices  9.05 us (37%)
  waiting for transfers between devices  8.05 us (33%)
  Pallas kernels  6.55 us (27%)
  other arithmetic  0.31 us (1%)
    ppermute x6, starting transfers between devices, shifted(): lax.ppermute(shard, axis, [(i, (i + by) % size) for i in range(size)])  9.05 us
    ppermute x6, waiting for transfers between devices, shifted(): lax.ppermute(shard, axis, [(i, (i + by) % size) for i in range(size)])  8.05 us
    pallas_call x5, Pallas kernels, call(): pl.pallas_call(kernel, out_shape=out_shape, in_specs=in_specs, compiler_p...  6.55 us
  transfers between devices with their start and end apart: 6, of which 3 were waited for; matrix products, arithmetic and copies ran while one was open for 1% of the time, Pallas kernels for 11%

commit v1 on v0

--- a/solution.py
+++ b/solution.py
@@ -10,6 +10,7 @@
 CB = 8
 RIM = 2
 SCALE = 16.0
+PIECES = 2
 
 
 VMEM = pl.BlockSpec(memory_space=pltpu.VMEM)
@@ -58,28 +59,43 @@
 
 
 def gather_kernel(rows_hbm, cols_hbm, tiles_hbm, owned_hbm, dense, owned, rim, to_diag, tiles, rows, cols, sems):
-    copies = [
-        pltpu.make_async_copy(rows_hbm, rows, sems.at[0]),
-        pltpu.make_async_copy(cols_hbm, cols, sems.at[1]),
-        pltpu.make_async_copy(tiles_hbm, tiles, sems.at[2]),
-        pltpu.make_async_copy(owned_hbm, owned, sems.at[3]),
+    n_tiles = tiles.shape[0]
+    bounds = [n_tiles * k // PIECES for k in range(PIECES + 1)]
+    index = [pltpu.make_async_copy(rows_hbm, rows, sems.at[0]), pltpu.make_async_copy(cols_hbm, cols, sems.at[1])]
+    pieces = [
+        pltpu.make_async_copy(tiles_hbm.at[pl.ds(lo, hi - lo)], tiles.at[pl.ds(lo, hi - lo)], sems.at[3 + k])
+        for k, (lo, hi) in enumerate(zip(bounds, bounds[1:]))
     ]
-    for copy in copies:
+    mine = pltpu.make_async_copy(owned_hbm, owned, sems.at[2])
+    for copy in index + pieces + [mine]:
         copy.start()
     dense[...] = jnp.zeros_like(dense)
-    for copy in copies[:3]:
+    for copy in index:
         copy.wait()
-    for t in range(tiles.shape[0]):
-        row, col = rows[0, 0, t], cols[0, 0, t]
-        dense[pl.ds(pl.multiple_of(row * BS, BS), BS), pl.ds(pl.multiple_of(col * BS, BS), BS)] = tiles[t]
-    copies[3].wait()
+    for k, copy in enumerate(pieces):
+        copy.wait()
+        for t in range(bounds[k], bounds[k + 1]):
+            row, col = rows[0, 0, t], cols[0, 0, t]
+            dense[pl.ds(pl.multiple_of(row * BS, BS), BS), pl.ds(pl.multiple_of(col * BS, BS), BS)] = tiles[t]
+    mine.wait()
+    to_diag[...] = transposed_dot(dense[:, rim_columns(2)], owned[...])
     rim[...] = owned[:RIM * BS, :]
-    to_diag[...] = transposed_dot(dense[:, rim_columns(2)], owned[...])
 
 
-def mirror_kernel(dense, owned, to_col, to_row):
-    to_row[...] = transposed_dot(dense[:, rim_columns(1)], owned[...])
-    to_col[...] = transposed_dot(dense[:, rim_columns(0)], owned[...])
+def early_kernel(dense, owned, to_col, to_row):
+    @pl.when(lax.axis_index("col") == 0)
+    def _():
+        to_row[...] = transposed_dot(dense[:, rim_columns(1)], owned[...])
+        to_col[...] = transposed_dot(dense[:, rim_columns(0)], owned[...])
+
+
+def late_kernel(dense, owned, early_col, early_row, to_col, to_row):
+    del early_col, early_row
+
+    @pl.when(lax.axis_index("col") != 0)
+    def _():
+        to_row[...] = transposed_dot(dense[:, rim_columns(1)], owned[...])
+        to_col[...] = transposed_dot(dense[:, rim_columns(0)], owned[...])
 
 
 def own_kernel(dense, owned, total, square):
@@ -95,10 +111,19 @@
     more[...] = total[...] + dot(dense[:, rim_columns(0)], beside[...]) + dot(dense[:, rim_columns(1)], below[...])
 
 
-def finish_kernel(total, dense, corner, from_row, from_col, out):
-    acc = total[...] + dot(dense[:, rim_columns(2)], corner[...])
-    out[RIM * BS:, :] = acc[RIM * BS:].astype(out.dtype)
-    out[:RIM * BS, :] = (acc[:RIM * BS] + from_row[...] + from_col[...]).astype(out.dtype)
+def bulk_kernel(total, dense, corner, from_row, lead, out, rest, sems):
+    rim_rows = RIM * BS
+    corner_columns = rim_columns(2)
+    copies = []
+    for k in range(1, CB // RIM):
+        rows = pl.ds(k * rim_rows, rim_rows)
+        here_rows = pl.ds((k - 1) * rim_rows, rim_rows)
+        rest[here_rows, :] = (total[rows, :] + dot(dense[rows, corner_columns], corner[...])).astype(rest.dtype)
+        copies.append(pltpu.make_async_copy(rest.at[here_rows], out.at[rows], sems.at[k - 1]))
+        copies[-1].start()
+    lead[...] = total[:rim_rows, :] + dot(dense[:rim_rows, corner_columns], corner[...]) + from_row[...]
+    for copy in copies:
+        copy.wait()
 
 
 def inner_body(orbitals, tiles, tile_rows, tile_cols):
@@ -117,10 +142,11 @@
             pltpu.VMEM(stored.shape, BF16),
             pltpu.SMEM(tile_rows.shape, jnp.int32),
             pltpu.SMEM(tile_cols.shape, jnp.int32),
-            pltpu.SemaphoreType.DMA((4,)),
+            pltpu.SemaphoreType.DMA((3 + PIECES,)),
         ],
     )
-    to_col, to_row = call(mirror_kernel, (part, part), (dense, owned))
+    early = call(early_kernel, (part, part), (dense, owned))
+    to_col, to_row = call(late_kernel, (part, part), (dense, owned, *early), input_output_aliases={2: 0, 3: 1})
     enc = lambda x: (x * SCALE).astype(jnp.float16)
     dec = lambda x: x.astype(F32) * (1 / SCALE)
     from_diag = shifted(enc(to_diag), "row", 1)
@@ -131,7 +157,12 @@
     from_col = shifted(enc(to_col + dec(from_diag)), "col", 1)
     total = call(own_kernel, whole, (dense, owned), scratch_shapes=[pltpu.VMEM((CB * BS, CB * BS), BF16)])
     total = call(beside_kernel, whole, (total, dense, beside, below))
-    out = call(finish_kernel, jax.ShapeDtypeStruct((CB * BS, occ), BF16), (total, dense, corner, dec(from_row), dec(from_col)))
+    lead, out = call(
+        bulk_kernel, (part, pltpu.HBM((CB * BS, occ), BF16)), (total, dense, corner, dec(from_row)),
+        out_specs=(VMEM, ANY),
+        scratch_shapes=[pltpu.VMEM(((CB - RIM) * BS, occ), BF16), pltpu.SemaphoreType.DMA((CB // RIM - 1,))],
+    )
+    out = lax.dynamic_update_slice(out, (lead + dec(from_col)).astype(BF16), (0, 0))
     return out.reshape(orbitals.shape)
 
 

time: 24.2 us -> 27.5 us (1.14)
  waiting for transfers between devices: 8.05 us -> 11.9 us
  starting transfers between devices: 9.05 us -> 8.06 us
  other arithmetic: 0.31 us -> 1.03 us
  Pallas kernels: 6.55 us -> 6.18 us
    ppermute x6, waiting for transfers between devices: 8.05 us -> 11.9 us  [shifted(): lax.ppermute(shard, axis, [(i, (i + by) % size) for i in range(size)])]
    ppermute x6, starting transfers between devices: 9.05 us -> 8.06 us  [shifted(): lax.ppermute(shard, axis, [(i, (i + by) % size) for i in range(size)])]
    dynamic_update_slice x0 -> x1, other arithmetic: none -> 0.78 us  [inner_body(): lax.dynamic_update_slice(out, (lead + dec(from_col)).astype(BF16), (0, 0))]
    pallas_call x5 -> x6, Pallas kernels: 6.55 us -> 6.18 us  [call(): pl.pallas_call(kernel, out_shape=out_shape, in_specs=in_specs, compiler_p...]
  transfers between devices with their start and end apart: 6 -> 6, of which waited for: 3 -> 6; matrix products, arithmetic and copies ran while one was open for 1% -> 1% of each run, Pallas kernels for 11% -> 14%
where the time goes in v1:
time: 27.5 us; the launch traced here: 27.3 us
  waiting for transfers between devices  11.9 us (43%)
  starting transfers between devices  8.06 us (29%)
  Pallas kernels  6.18 us (22%)
  other arithmetic  1.03 us (4%)
    ppermute x6, waiting for transfers between devices, shifted(): lax.ppermute(shard, axis, [(i, (i + by) % size) for i in range(size)])  11.9 us
    ppermute x6, starting transfers between devices, shifted(): lax.ppermute(shard, axis, [(i, (i + by) % size) for i in range(size)])  8.06 us
    pallas_call x6, Pallas kernels, call(): pl.pallas_call(kernel, out_shape=out_shape, in_specs=in_specs, compiler_p...  6.18 us
    dynamic_update_slice x1, other arithmetic, inner_body(): lax.dynamic_update_slice(out, (lead + dec(from_col)).astype(BF16), (0, 0))  0.78 us
  transfers between devices with their start and end apart: 6, of which 6 were waited for; matrix products, arithmetic and copies ran while one was open for 1% of the time, Pallas kernels for 14%

profile of v1, /device:TPU:0, one launch (start us, length us, event | category | flops | bytes accessed | tf_op | source)
XLA Modules:
  0.0 27.3 jit_solution(9243007360314203593)
XLA Ops:
  0.0 2.3 %shard_map.46 = (bf16[1024,1792]{1,0:T(8,128)(2,1)S(1)}, bf16[1024,512]{1,0:T(8,128)(2,1)S(1)}, bf16[256,512]{1,0:T(8,128)(2,1)S(1)}, f32[256,512]{1,0:T(8,128)S(1)}) custom-call(s32[1,1,60]{2,1,0:T(1,128)} %rows_hbm.1, s32[1,1,60]{2,1,0:T(1,128)} %cols_hbm.1, bf16[60,128,128]{2,1,0:T(8,128)(2,1)} %bitcast.7, bf16[1024,512]{1,0:T(8,128)(2,1)} %bitcast.8), custom_call_target="tpu_custom_call" | custom-call | tf_op jit(solution)/shard_map/pallas_call | solution.py:39
  2.4 6.1 %collective-permute-start = (bf16[256,512]{1,0:T(8,128)(2,1)S(1)}, bf16[256,512]{1,0:T(8,128)(2,1)S(1)}, u32[]{:S(2)}, u32[]{:S(2)}) collective-permute-start(bf16[256,512]{1,0:T(8,128)(2,1)S(1)} %get-tuple-element.17), channel_id=1, source_target_pairs={{0,7},{1,0},{2,1},{3,2},{4,3},{5,4},{6,5},{7,6},{8,15},{9,8},{10,9... | collective-permute-start | bytes 786440 | tf_op jit(solution)/shard_map/ppermute | solution.py:23
  8.5 0.1 collective-permute-start.4
  8.5 1.7 %collective-permute-start.1 = (bf16[256,512]{1,0:T(8,128)(2,1)S(1)}, bf16[256,512]{1,0:T(8,128)(2,1)S(1)}, u32[]{:S(2)}, u32[]{:S(2)}) collective-permute-start(bf16[256,512]{1,0:T(8,128)(2,1)S(1)} %get-tuple-element.17), channel_id=1, source_target_pairs={{0,24},{8,0},{16,8},{24,16},{1,25},{9,1},{17,9},{25,17},{2,26},{10... | collective-permute-start | bytes 786440 | tf_op jit(solution)/shard_map/ppermute | solution.py:23
  10.3 0.7 %shard_map.49 = (f32[256,512]{1,0:T(8,128)S(1)}, f32[256,512]{1,0:T(8,128)S(1)}) custom-call(bf16[1024,1792]{1,0:T(8,128)(2,1)S(1)} %get-tuple-element.15.dense, bf16[1024,512]{1,0:T(8,128)(2,1)S(1)} %get-tuple-element.16.owned), custom_call_target="tpu_custom_call" | custom-call | tf_op jit(solution)/shard_map/pallas_call | solution.py:39
  11.1 0.1 collective-permute-start.3
  11.1 2.8 %collective-permute-done.beside = bf16[256,512]{1,0:T(8,128)(2,1)S(1)} collective-permute-done((bf16[256,512]{1,0:T(8,128)(2,1)S(1)}, bf16[256,512]{1,0:T(8,128)(2,1)S(1)}, u32[]{:S(2)}, u32[]{:S(2)}) %collective-permute-start) | collective-permute-done | bytes 262176 | tf_op jit(solution)/shard_map/ppermute | solution.py:23
  14.0 0.1 collective-permute-start.2
  14.1 1.2 %collective-permute-done.4 = f16[256,512]{1,0:T(8,128)(2,1)S(1)} collective-permute-done((f16[256,512]{1,0:T(8,128)(2,1)S(1)}, f16[256,512]{1,0:T(8,128)(2,1)S(1)}, u32[]{:S(2)}, u32[]{:S(2)}) %collective-permute-start.4) | collective-permute-done | bytes 262176 | tf_op jit(solution)/shard_map/ppermute | solution.py:23
  15.3 0.1 multiply_convert_fusion
  15.4 0.1 collective-permute-start.5
  15.5 1.3 %shard_map.47.total = f32[1024,512]{1,0:T(8,128)S(1)} custom-call(bf16[1024,1792]{1,0:T(8,128)(2,1)S(1)} %get-tuple-element.15.dense, bf16[1024,512]{1,0:T(8,128)(2,1)S(1)} %get-tuple-element.16.owned), custom_call_target="tpu_custom_call" | custom-call | tf_op jit(solution)/shard_map/pallas_call | solution.py:39
  16.7 0.2 collective-permute-done.1.below
  17.0 0.7 %shard_map.48.total = f32[1024,512]{1,0:T(8,128)S(1)} custom-call(f32[1024,512]{1,0:T(8,128)S(1)} %shard_map.47.total, bf16[1024,1792]{1,0:T(8,128)(2,1)S(1)} %get-tuple-element.15.dense, bf16[256,512]{1,0:T(8,128)(2,1)S(1)} %collective-permute-done.beside, bf16[256,512]{1,0:T(8,128)(2,1)S(1)} %collective-permute-done.1.below), custom_call_target="tpu_custom_call" | custom-call | tf_op jit(solution)/shard_map/pallas_call | solution.py:39
  17.7 3.3 %collective-permute-done.3 = f16[256,512]{1,0:T(8,128)(2,1)S(1)} collective-permute-done((f16[256,512]{1,0:T(8,128)(2,1)S(1)}, f16[256,512]{1,0:T(8,128)(2,1)S(1)}, u32[]{:S(2)}, u32[]{:S(2)}) %collective-permute-start.3) | collective-permute-done | bytes 262176 | tf_op jit(solution)/shard_map/ppermute | solution.py:23
  20.9 0.1 convert_multiply_fusion.from_row
  21.0 0.8 %collective-permute-done.2.corner = bf16[256,512]{1,0:T(8,128)(2,1)S(1)} collective-permute-done((bf16[256,512]{1,0:T(8,128)(2,1)S(1)}, bf16[256,512]{1,0:T(8,128)(2,1)S(1)}, u32[]{:S(2)}, u32[]{:S(2)}) %collective-permute-start.2) | collective-permute-done | bytes 262176 | tf_op jit(solution)/shard_map/ppermute | solution.py:23
  21.8 1.1 %shard_map.51 = (f32[256,512]{1,0:T(8,128)S(1)}, bf16[1024,512]{1,0:T(8,128)(2,1)}) custom-call(f32[1024,512]{1,0:T(8,128)S(1)} %shard_map.48.total, bf16[1024,1792]{1,0:T(8,128)(2,1)S(1)} %get-tuple-element.15.dense, bf16[256,512]{1,0:T(8,128)(2,1)S(1)} %collective-permute-done.2.corner, f32[256,512]{1,0:T(8,128)S(1)} %convert_multiply_fusion.from_row), custom_call_target="tpu_custom_call" | custom-call | tf_op jit(solution)/shard_map/pallas_call | solution.py:39
  22.9 3.6 %collective-permute-done.5 = f16[256,512]{1,0:T(8,128)(2,1)S(1)} collective-permute-done((f16[256,512]{1,0:T(8,128)(2,1)S(1)}, f16[256,512]{1,0:T(8,128)(2,1)S(1)}, u32[]{:S(2)}, u32[]{:S(2)}) %collective-permute-start.5) | collective-permute-done | bytes 262176 | tf_op jit(solution)/shard_map/ppermute | solution.py:23
  26.5 0.8 %fusion.1 = bf16[1,1,1024,512]{3,2,1,0:T(8,128)(2,1)} fusion(bf16[1,1,1024,512]{3,2,1,0:T(8,128)(2,1)} %bitcast.9, f32[256,512]{1,0:T(8,128)S(1)} %get-tuple-element.22, f16[256,512]{1,0:T(8,128)(2,1)S(1)} %collective-permute-done.5), kind=kLoop, calls=%fused_computation.6 | loop fusion | flops 524288 | bytes 1048576 | tf_op jit(solution)/shard_map/dynamic_update_slice | solution.py:165
  (3 shorter events, 0.1 us)
Async XLA Ops:
  2.4 11.6 %collective-permute-start = (bf16[256,512]{1,0:T(8,128)(2,1)S(1)}, bf16[256,512]{1,0:T(8,128)(2,1)S(1)}, u32[]{:S(2)}, u32[]{:S(2)}) collective-permute-start(bf16[256,512]{1,0:T(8,128)(2,1)S(1)} %get-tuple-element.17), channel_id=1, source_target_pairs={{0,7},{1,0},{2,1},{3,2},{4,3},{5,4},{6,5},{7,6},{8,15},{9,8},{10,9... | collective-permute-start | bytes 786440 | tf_op jit(solution)/shard_map/ppermute | solution.py:23
  8.5 6.8 %collective-permute-start.4 = (f16[256,512]{1,0:T(8,128)(2,1)S(1)}, f16[256,512]{1,0:T(8,128)(2,1)S(1)}, u32[]{:S(2)}, u32[]{:S(2)}) collective-permute-start(f16[256,512]{1,0:T(8,128)(2,1)S(1)} %multiply_convert_fusion.1), channel_id=1, source_target_pairs={{0,8},{8,16},{16,24},{24,0},{1,9},{9,17},{17,25},{25,1},{2,10},{10... | collective-permute-start | bytes 786440 | tf_op jit(solution)/shard_map/ppermute | solution.py:23
  8.5 8.4 %collective-permute-start.1 = (bf16[256,512]{1,0:T(8,128)(2,1)S(1)}, bf16[256,512]{1,0:T(8,128)(2,1)S(1)}, u32[]{:S(2)}, u32[]{:S(2)}) collective-permute-start(bf16[256,512]{1,0:T(8,128)(2,1)S(1)} %get-tuple-element.17), channel_id=1, source_target_pairs={{0,24},{8,0},{16,8},{24,16},{1,25},{9,1},{17,9},{25,17},{2,26},{10... | collective-permute-start | bytes 786440 | tf_op jit(solution)/shard_map/ppermute | solution.py:23
  11.1 9.8 %collective-permute-start.3 = (f16[256,512]{1,0:T(8,128)(2,1)S(1)}, f16[256,512]{1,0:T(8,128)(2,1)S(1)}, u32[]{:S(2)}, u32[]{:S(2)}) collective-permute-start(f16[256,512]{1,0:T(8,128)(2,1)S(1)} %multiply_convert_fusion.2), channel_id=1, source_target_pairs={{0,8},{8,16},{16,24},{24,0},{1,9},{9,17},{17,25},{25,1},{2,10},{10... | collective-permute-start | bytes 786440 | tf_op jit(solution)/shard_map/ppermute | solution.py:23
  14.0 7.8 %collective-permute-start.2 = (bf16[256,512]{1,0:T(8,128)(2,1)S(1)}, bf16[256,512]{1,0:T(8,128)(2,1)S(1)}, u32[]{:S(2)}, u32[]{:S(2)}) collective-permute-start(bf16[256,512]{1,0:T(8,128)(2,1)S(1)} %collective-permute-done.beside), channel_id=1, source_target_pairs={{0,24},{8,0},{16,8},{24,16},{1,25},{9,1},{17,9},{25,17},{2,26},{10... | collective-permute-start | bytes 786440 | tf_op jit(solution)/shard_map/ppermute | solution.py:23
  15.4 11.1 %collective-permute-start.5 = (f16[256,512]{1,0:T(8,128)(2,1)S(1)}, f16[256,512]{1,0:T(8,128)(2,1)S(1)}, u32[]{:S(2)}, u32[]{:S(2)}) collective-permute-start(f16[256,512]{1,0:T(8,128)(2,1)S(1)} %multiply_convert_fusion), channel_id=1, source_target_pairs={{0,1},{1,2},{2,3},{3,4},{4,5},{5,6},{6,7},{7,0},{8,9},{9,10},{10,1... | collective-permute-start | bytes 786440 | tf_op jit(solution)/shard_map/ppermute | solution.py:23
